TPU v7x, 128 devices: a whole 4x4x4 slice. The times are simulated.
128 devices in a mesh: rows: 8 (over z_hi, y), cols: 16 (over z_lo, x, core).
Axes of the slice: x: 4, y: 4, z: 4 (z_hi: 2, z_lo: 2; z = z_hi * 2 + z_lo), core: 2. Of those that a mesh axis runs over, the one named last changes fastest.
Arguments:
- dosage: int32 [512, 24576], P('cols', 'rows'), may hold values from 0 to 2
- present: int32 [512, 24576], P('cols', 'rows'), may hold values from 0 to 1, as said below
- components: float32 [32, 24576], P(None, 'rows'), may hold values from -8 to 8
Outputs:
- kinship: float32 [24576, 24576], P('rows', 'cols')
Inputs may be any that keep to these rules, and one draw needn't show every extreme that they name: `present`: markers whose index is a multiple of 8 are observed for every person.
All inputs are finite; a program needn't handle non-finite values.
Results may differ from a plain program's by a relative error of at most 0.0036.
Values may be sent and summed in bfloat16 or wider, within the bound.
A program may use at most 128 MiB of HBM per device.

v0:
```python
import jax
import jax.numpy as jnp
from jax import lax
from jax.sharding import PartitionSpec as P


def broadcast(block, axis, holder):
    block = jnp.where(lax.axis_index(axis) == holder, block, jnp.zeros_like(block))
    return lax.psum(block, axis)


def solve_normal(gram, moment):
    width = gram.shape[0]
    index_col = jnp.arange(width, dtype=jnp.int32)[:, None]
    columns = []
    for j in range(width):
        column = gram[:, j, :]
        if j > 0:
            stacked = jnp.stack(columns, axis=1)
            column = column - jnp.sum(stacked * stacked[j][None, :, :], axis=1)
        pivot = jnp.sqrt(column[j])
        columns.append(jnp.where(index_col >= j, column / pivot[None, :], jnp.zeros_like(column)))
    factor = jnp.stack(columns, axis=1)
    forward = []
    for j in range(width):
        value = moment[j]
        for k in range(j):
            value = value - factor[j, k] * forward[k]
        forward.append(value / factor[j, j])
    backward = [None] * width
    for j in range(width - 1, -1, -1):
        value = forward[j]
        for k in range(j + 1, width):
            value = value - factor[k, j] * backward[k]
        backward[j] = value / factor[j, j]
    return jnp.stack(backward, axis=0)


def per_device(dosage, present, components):
    people = components.shape[1]
    design = jnp.concatenate([jnp.ones((1, people), jnp.float32), components], axis=0)
    width = design.shape[0]
    observed = present.astype(jnp.float32)
    counts = dosage.astype(jnp.float32)
    target = 0.5 * counts * observed
    outer_rows = (design[:, None, :] * design[None, :, :]).reshape(width * width, people)
    gram_part = jnp.dot(
        outer_rows, observed.T, precision=lax.Precision.HIGHEST, preferred_element_type=jnp.float32
    )
    moment_part = jnp.dot(
        design, target.T, precision=lax.Precision.HIGHEST, preferred_element_type=jnp.float32
    )
    gram_flat, moment = lax.psum((gram_part, moment_part), "rows")
    markers_here = observed.shape[0]
    gram = gram_flat.reshape(width, width, markers_here)
    coef = solve_normal(gram, moment)
    fitted = jnp.dot(
        coef.T, design, precision=lax.Precision.HIGHEST, preferred_element_type=jnp.float32
    )
    freq = jnp.clip(fitted, 0.01, 0.99)
    resid = observed * (counts - 2.0 * freq)
    sdev = observed * jnp.sqrt(freq * (1.0 - freq))
    panel = jnp.stack([resid, sdev]).astype(jnp.bfloat16)
    ratio = lax.axis_size("cols") // lax.axis_size("rows")
    column_width = people // ratio
    col_index = lax.axis_index("cols")
    col_start = col_index % ratio * column_width
    owner = col_index // ratio
    contract = (((0,), (0,)), ((), ()))
    full_rows = lax.all_gather(panel, "cols", axis=1, tiled=True)
    own_part = lax.dynamic_slice_in_dim(full_rows, col_start, column_width, 2)
    full_cols = broadcast(own_part, "rows", owner)
    numer = lax.dot_general(
        full_rows[0], full_cols[0], contract, preferred_element_type=jnp.float32
    )
    denom = lax.dot_general(
        full_rows[1], full_cols[1], contract, preferred_element_type=jnp.float32
    )
    return numer / (4.0 * denom)


def solution(mesh):
    placed = (P("cols", "rows"), P("cols", "rows"), P(None, "rows"))
    return jax.shard_map(
        per_device, mesh=mesh, in_specs=placed, out_specs=P("rows", "cols"), check_vma=False
    )
```

profile of v0, /device:TPU:0, one launch (start us, length us, event | category | flops | bytes accessed | tf_op | source)
XLA Modules:
  0.0 338.4 jit_solution(12750329239006864521)
XLA Ops:
  6.5 1.0 concatenate.3
  7.6 8.0 %broadcast_multiply_fusion = f32[33,33,3072]{2,1,0:T(8,128)} fusion(f32[33,3072]{1,0:T(8,128)S(1)} %concatenate.3), kind=kLoop, calls=%fused_computation.1 | loop fusion | flops 3345408 | bytes 13787136 | tf_op jit(solution)/shard_map/mul | solution.py:46
  15.6 10.5 %mul.11354 = f32[1089,3072]{1,0:T(8,128)} reshape(f32[33,33,3072]{2,1,0:T(8,128)} %broadcast_multiply_fusion) | data formatting | bytes 26763264 | tf_op jit(solution)/shard_map/mul | solution.py:46
  26.1 14.2 %fusion.8 = f32[1089,32]{0,1:T(8,128)S(1)} fusion(f32[1089,3072]{1,0:T(8,128)} %mul.11354, s32[32,3072]{1,0:T(8,128)S(1)} %copy-done.1), kind=kOutput, calls=%fused_computation.550 | convolution fusion | flops 1284734976 | bytes 13914240 | tf_op jit(solution)/shard_map/dot_general | solution.py:47
  40.6 1.2 copy.48
  43.4 42.9 %psum.21 = f32[33,32]{1,0:T(8,128)S(1)} all-reduce(f32[33,32]{1,0:T(8,128)S(1)} %fusion.4), channel_id=1, replica_groups=mesh['rows'=8,'cols'=16] {'rows'}, use_global_device_ids=true, to_apply=%region_0.0 | all-reduce | flops 1056 | bytes 8448 | tf_op jit(solution)/shard_map/psum | solution.py:53
  86.4 44.7 %all-reduce.4.cloned.1.call-done = f32[33,33,32]{2,0,1:T(8,128)} async-done(((f32[33,33,32]{2,0,1:T(8,128)}), f32[33,33,32]{2,0,1:T(8,128)}) %all-reduce.4.cloned.1.call-update) | async-done | bytes 139408 | tf_op jit(solution)/shard_map/psum | solution.py:53
  131.1 0.8 fusion.113
  131.8 0.7 bitcast_divide_fusion.1
  132.6 0.7 constant_dynamic-update-slice_fusion.517
  133.3 0.8 constant_dynamic-update-slice_fusion.454
  134.2 0.7 bitcast_subtract_fusion.59
  135.0 0.8 constant_dynamic-update-slice_fusion.79
  135.9 0.7 bitcast_subtract_fusion.58
  136.7 0.8 constant_dynamic-update-slice_fusion.514
  138.4 0.8 constant_dynamic-update-slice_fusion.513
  140.1 0.8 constant_dynamic-update-slice_fusion.512
  141.8 0.8 constant_dynamic-update-slice_fusion.511
  143.5 0.8 constant_dynamic-update-slice_fusion.510
  145.2 0.8 constant_dynamic-update-slice_fusion.509
  146.9 0.8 constant_dynamic-update-slice_fusion.508
  147.8 0.7 bitcast_subtract_fusion.44
  148.6 0.8 constant_dynamic-update-slice_fusion.507
  157.1 0.8 fusion.144
  158.4 0.8 subtract_divide_fusion
  159.3 0.7 fusion.11
  160.1 0.8 pad_maximum_fusion
  161.2 40.2 %all-gather.2.cloned.1.call-done = bf16[2,512,3072]{2,1,0:T(8,128)(2,1)} async-done(((bf16[2,32,3072]{2,1,0:T(8,128)(2,1)}), bf16[2,512,3072]{2,1,0:T(8,128)(2,1)}) %all-gather.2.cloned.1.call-update) | async-done | bytes 6291472 | tf_op jit(solution)/shard_map/all_gather | solution.py:70
  201.4 4.1 %dynamic-slice_select_fusion = bf16[2,512,1536]{2,1,0:T(8,128)(2,1)} fusion(bf16[2,512,3072]{2,1,0:T(8,128)(2,1)} %all-gather.2.cloned.1.call-done, s32[]{:T(128)S(6)} %select_n.281, pred[]{:T(512)S(6)} %eq.5), kind=kLoop, calls=%fused_computation.6 | loop fusion | flops 1572864 | bytes 6291461 | tf_op jit(solution)/shard_map/jit(_where)/select_n | solution.py:8
  205.5 100.6 %all-reduce.6.cloned.1.call-done = bf16[2,512,1536]{2,1,0:T(8,128)(2,1)} async-done(((bf16[2,512,1536]{2,1,0:T(8,128)(2,1)}), bf16[2,512,1536]{2,1,0:T(8,128)(2,1)}) %all-reduce.6.cloned.1.call-update) | async-done | bytes 3145744 | tf_op jit(solution)/shard_map/psum | solution.py:9
  306.1 11.7 %fusion = f32[3072,1536]{1,0:T(8,128)} fusion(bf16[2,512,3072]{2,1,0:T(8,128)(2,1)} %all-gather.2.cloned.1.call-done, bf16[2,512,1536]{2,1,0:T(8,128)(2,1)} %all-reduce.6.cloned.1.call-done), kind=kOutput, calls=%fused_computation.5 | convolution fusion | flops 4831838208 | bytes 23592960 | tf_op jit(solution)/shard_map/dot_general | solution.py:73
  317.8 14.1 %multiply_divide_fusion = f32[3072,1536]{1,0:T(8,128)} fusion(f32[3072,1536]{1,0:T(8,128)} %fusion, bf16[2,512,3072]{2,1,0:T(8,128)(2,1)} %all-gather.2.cloned.1.call-done, bf16[2,512,1536]{2,1,0:T(8,128)(2,1)S(1)} %copy-done.4), kind=kOutput, calls=%fused_computation | convolution fusion | flops 4841275392 | bytes 42467328 | tf_op jit(solution)/shard_map/dot_general | solution.py:76
  (297 shorter events, 15.0 us)
Async XLA Ops:
  6.5 124.5 %all-reduce.4.cloned.1.call-start = ((), (), s32[]{:S(2)}) async-start(), calls=%async_computation | async-start | bytes 1351680 | tf_op jit(solution)/shard_map/psum | solution.py:53
  15.6 10.6 %copy-start.1 = (s32[32,3072]{1,0:T(8,128)S(1)}, s32[32,3072]{1,0:T(8,128)}, u32[]{:S(2)}) copy-start(s32[32,3072]{1,0:T(8,128)} %param.4) | copy-start | bytes 1179652
  26.1 16.1 %copy-start = (f32[32,3072]{1,0:T(8,128)S(1)}, f32[32,3072]{1,0:T(8,128)}, u32[]{:S(2)}) copy-start(f32[32,3072]{1,0:T(8,128)} %param.5) | copy-start | bytes 1179652
  26.1 16.1 %copy-start.3 = (s32[32,3072]{1,0:T(8,128)S(1)}, s32[32,3072]{1,0:T(8,128)}, u32[]{:S(2)}) copy-start(s32[32,3072]{1,0:T(8,128)} %param.3) | copy-start | bytes 1179652
  41.8 159.6 %all-gather.2.cloned.1.call-start = ((), (), s32[]{:S(2)}) async-start(), calls=%async_computation.1 | async-start | bytes 6684672 | tf_op jit(solution)/shard_map/all_gather | solution.py:70
  131.1 18.4 %copy-start.2 = (f32[33,33,32]{2,0,1:T(8,128)S(1)}, f32[33,33,32]{2,0,1:T(8,128)}, u32[]{:S(2)}) copy-start(f32[33,33,32]{2,0,1:T(8,128)} %all-reduce.4.cloned.1.call-done) | copy-start | bytes 418180
  160.9 145.2 %all-reduce.6.cloned.1.call-start = ((), (), s32[]{:S(2)}) async-start(), calls=%async_computation.2 | async-start | bytes 6291456 | tf_op jit(solution)/shard_map/psum | solution.py:9
  306.1 11.7 %copy-start.4 = (bf16[2,512,1536]{2,1,0:T(8,128)(2,1)S(1)}, bf16[2,512,1536]{2,1,0:T(8,128)(2,1)}, u32[]{:S(2)}) copy-start(bf16[2,512,1536]{2,1,0:T(8,128)(2,1)} %all-reduce.6.cloned.1.call-done) | copy-start | bytes 9437188
Sparse Core Ops, SparseCore 0:
  41.9 89.0 all-reduce.3
  161.0 40.3 all-gather.1
  205.6 100.4 all-reduce.5
where the time goes:
time: 340 us; the launch traced here: 338 us
  waiting for transfers between devices  186 us (55%)
  blocking collectives  42.9 us (13%)
  matrix products  41.3 us (12%)
  other arithmetic  37.7 us (11%)
  local copies, waits for them, and re-layouts  16.1 us (5%)
  between operations  14.5 us (4%)
    psum x1, waiting for transfers between devices, broadcast(): return lax.psum(block, axis)  101 us
    psum x1, waiting for transfers between devices, per_device(): gram_flat, moment = lax.psum((gram_part, moment_part), 'rows')  44.7 us
    psum x1, blocking collectives, per_device(): gram_flat, moment = lax.psum((gram_part, moment_part), 'rows')  42.9 us
    all_gather x1, waiting for transfers between devices, per_device(): full_rows = lax.all_gather(panel, 'cols', axis=1, tiled=True)  40.2 us
    dot_general x1, matrix products, per_device(): jnp.dot(outer_rows, observed.T, precision=lax.Precision.HIGHEST, preferre...  14.2 us
    dot_general x1, matrix products, per_device(): lax.dot_general(full_rows[1], full_cols[1], contract, preferred_element_t...  14.1 us
    dot_general x1, matrix products, per_device(): lax.dot_general(full_rows[0], full_cols[0], contract, preferred_element_t...  11.7 us
    mul x1, local copies, waits for them, and re-layouts, per_device(): design[:, None, :] * design[None, :, :]  10.5 us
  transfers between devices with their start and end apart: 3, of which 3 were waited for; matrix products, arithmetic and copies ran while one was open for 0% of the time, Pallas kernels for 0%

commit v1 on v0

--- a/solution.py
+++ b/solution.py
@@ -67,7 +67,9 @@
     col_start = col_index % ratio * column_width
     owner = col_index // ratio
     contract = (((0,), (0,)), ((), ()))
-    full_rows = lax.all_gather(panel, "cols", axis=1, tiled=True)
+    full_rows = jnp.concatenate(
+        lax.all_to_all(jnp.stack([panel] * lax.axis_size("cols")), "cols", 0, 0), axis=1
+    )
     own_part = lax.dynamic_slice_in_dim(full_rows, col_start, column_width, 2)
     full_cols = broadcast(own_part, "rows", owner)
     numer = lax.dot_general(

time: 340 us -> 384 us (1.13)
  waiting for transfers between devices: 186 us -> 221 us
  local copies, waits for them, and re-layouts: 16.1 us -> 30.7 us
  other arithmetic: 37.7 us -> 27.3 us
  starting transfers between devices: 0.31 us -> 4.89 us
    all_to_all x0 -> x1, waiting for transfers between devices: none -> 84.1 us  [per_device(): lax.all_to_all(jnp.stack([panel] * lax.axis_size('cols')), 'cols', 0, 0)]
    all_gather x1 -> x0, waiting for transfers between devices: 40.2 us -> none  [per_device(): full_rows = lax.all_gather(panel, 'cols', axis=1, tiled=True)]
    psum x1, waiting for transfers between devices: 101 us -> 92.6 us  [broadcast(): return lax.psum(block, axis)]
    slice x0 -> x1, local copies, waits for them, and re-layouts: none -> 5.19 us  [per_device(): full_rows[1]]
    all_to_all x0 -> x1, starting transfers between devices: none -> 4.63 us  [per_device(): lax.all_to_all(jnp.stack([panel] * lax.axis_size('cols')), 'cols', 0, 0)]
    unnamed x32, other arithmetic: 10.3 us -> 5.94 us
  transfers between devices with their start and end apart: 3 -> 3, of which waited for: 3 -> 3; matrix products, arithmetic and copies ran while one was open for 0% -> 2% of each run, Pallas kernels for 0% -> 0%
where the time goes in v1:
time: 384 us; the launch traced here: 383 us
  waiting for transfers between devices  221 us (58%)
  blocking collectives  42.9 us (11%)
  matrix products  40.4 us (11%)
  local copies, waits for them, and re-layouts  30.7 us (8%)
  other arithmetic  27.3 us (7%)
  between operations  15 us (4%)
  starting transfers between devices  4.89 us (1%)
    psum x1, waiting for transfers between devices, broadcast(): return lax.psum(block, axis)  92.6 us
    all_to_all x1, waiting for transfers between devices, per_device(): lax.all_to_all(jnp.stack([panel] * lax.axis_size('cols')), 'cols', 0, 0)  84.1 us
    psum x1, waiting for transfers between devices, per_device(): gram_flat, moment = lax.psum((gram_part, moment_part), 'rows')  44.7 us
    psum x1, blocking collectives, per_device(): gram_flat, moment = lax.psum((gram_part, moment_part), 'rows')  42.9 us
    dot_general x1, matrix products, per_device(): jnp.dot(outer_rows, observed.T, precision=lax.Precision.HIGHEST, preferre...  14.2 us
    dot_general x1, matrix products, per_device(): lax.dot_general(full_rows[1], full_cols[1], contract, preferred_element_t...  13.2 us
    dot_general x1, matrix products, per_device(): lax.dot_general(full_rows[0], full_cols[0], contract, preferred_element_t...  11.6 us
    mul x1, local copies, waits for them, and re-layouts, per_device(): design[:, None, :] * design[None, :, :]  10.5 us
  transfers between devices with their start and end apart: 3, of which 3 were waited for; matrix products, arithmetic and copies ran while one was open for 2% of the time, Pallas kernels for 0%

profile of v1, /device:TPU:0, one launch (start us, length us, event | category | flops | bytes accessed | tf_op | source)
XLA Modules:
  0.0 382.6 jit_solution(11348516062546511094)
XLA Ops:
  6.5 1.0 concatenate.6
  7.6 8.0 %broadcast_multiply_fusion = f32[33,33,3072]{2,1,0:T(8,128)} fusion(f32[33,3072]{1,0:T(8,128)S(1)} %concatenate.6), kind=kLoop, calls=%fused_computation.1 | loop fusion | flops 3345408 | bytes 13787136 | tf_op jit(solution)/shard_map/mul | solution.py:46
  15.6 10.5 %mul.11354 = f32[1089,3072]{1,0:T(8,128)} reshape(f32[33,33,3072]{2,1,0:T(8,128)} %broadcast_multiply_fusion) | data formatting | bytes 26763264 | tf_op jit(solution)/shard_map/mul | solution.py:46
  26.1 14.2 %fusion.8 = f32[1089,32]{0,1:T(8,128)S(1)} fusion(f32[1089,3072]{1,0:T(8,128)} %mul.11354, s32[32,3072]{1,0:T(8,128)S(1)} %copy-done.2), kind=kOutput, calls=%fused_computation.548 | convolution fusion | flops 1284734976 | bytes 13914240 | tf_op jit(solution)/shard_map/dot_general | solution.py:47
  40.5 1.2 copy.71
  42.8 0.6 slice.4600
  43.4 42.9 %psum.21 = f32[33,32]{1,0:T(8,128)S(1)} all-reduce(f32[33,32]{1,0:T(8,128)S(1)} %fusion.4), channel_id=1, replica_groups=mesh['rows'=8,'cols'=16] {'rows'}, use_global_device_ids=true, to_apply=%region_0.0 | all-reduce | flops 1056 | bytes 8448 | tf_op jit(solution)/shard_map/psum | solution.py:53
  86.3 44.7 %all-reduce.4.cloned.1.call-done = f32[33,33,32]{2,0,1:T(8,128)} async-done(((f32[33,33,32]{2,0,1:T(8,128)}), f32[33,33,32]{2,0,1:T(8,128)}) %all-reduce.4.cloned.1.call-update) | async-done | bytes 139408 | tf_op jit(solution)/shard_map/psum | solution.py:53
  131.1 0.8 fusion.113
  131.8 0.7 bitcast_divide_fusion.1
  132.6 0.7 constant_dynamic-update-slice_fusion.517
  133.3 0.8 constant_dynamic-update-slice_fusion.454
  134.2 0.7 bitcast_subtract_fusion.59
  135.0 0.8 constant_dynamic-update-slice_fusion.79
  135.9 0.7 bitcast_subtract_fusion.58
  136.7 0.8 constant_dynamic-update-slice_fusion.514
  137.6 0.7 bitcast_subtract_fusion.56
  138.5 0.8 constant_dynamic-update-slice_fusion.513
  139.3 0.7 bitcast_subtract_fusion.54
  149.1 0.8 fusion.144
  150.5 0.8 subtract_divide_fusion
  151.4 0.7 fusion.11
  152.2 3.5 stack.170
  155.7 4.6 %all-to-all-start = ((bf16[16,2,32,3072]{3,2,1,0:T(8,128)(2,1)}), bf16[16,2,32,3072]{3,2,1,0:T(8,128)(2,1)}, u32[]{:S(2)}, u32[]{:S(2)}) async-start(bf16[16,2,32,3072]{3,2,1,0:T(8,128)(2,1)} %stack.170), calls=%async_computation | async-start | bytes 12582912 | tf_op jit(solution)/shard_map/all_to_all | solution.py:71
  160.6 84.1 %all-to-all-done = bf16[16,2,32,3072]{3,2,1,0:T(8,128)(2,1)} async-done(((bf16[16,2,32,3072]{3,2,1,0:T(8,128)(2,1)}), bf16[16,2,32,3072]{3,2,1,0:T(8,128)(2,1)}, u32[]{:S(2)}, u32[]{:S(2)}) %all-to-all-start) | async-done | bytes 6291488 | tf_op jit(solution)/shard_map/all_to_all | solution.py:71
  244.7 3.2 copy.151
  247.9 2.7 copy-done
  250.6 2.5 dynamic-slice_select_fusion
  253.1 5.2 %fusion.1262 = (bf16[1,16,32,3072]{3,2,1,0:T(8,128)(2,1)S(1)}, bf16[1,16,32,3072]{3,2,1,0:T(8,128)(2,1)}) fusion(bf16[2,16,32,3072]{3,2,1,0:T(8,128)(2,1)} %bitcast.7585), kind=kLoop, calls=%fused_computation.3087 | loop fusion | bytes 12582912 | tf_op jit(solution)/shard_map/slice | solution.py:79
  258.3 92.6 %all-reduce.6.cloned.1.call-done = bf16[2,512,1536]{2,1,0:T(8,128)(2,1)} async-done(((bf16[2,512,1536]{2,1,0:T(8,128)(2,1)}), bf16[2,512,1536]{2,1,0:T(8,128)(2,1)}) %all-reduce.6.cloned.1.call-update) | async-done | bytes 3145744 | tf_op jit(solution)/shard_map/psum | solution.py:9
  350.9 11.6 %fusion = f32[3072,1536]{1,0:T(8,128)} fusion(bf16[512,3072]{1,0:T(8,128)(2,1)} %bitcast.7587, bf16[2,512,1536]{2,1,0:T(8,128)(2,1)} %all-reduce.6.cloned.1.call-done), kind=kOutput, calls=%fused_computation.6 | convolution fusion | flops 4831838208 | bytes 23592960 | tf_op jit(solution)/shard_map/dot_general | solution.py:75
  362.6 13.2 %multiply_divide_fusion = f32[3072,1536]{1,0:T(8,128)} fusion(f32[3072,1536]{1,0:T(8,128)} %fusion, bf16[512,3072]{1,0:T(8,128)(2,1)S(1)} %bitcast.7586, bf16[2,512,1536]{2,1,0:T(8,128)(2,1)S(1)} %copy-done.5), kind=kOutput, calls=%fused_computation | convolution fusion | flops 4841275392 | bytes 42467328 | tf_op jit(solution)/shard_map/dot_general | solution.py:78
  (301 shorter events, 10.5 us)
Async XLA Ops:
  6.5 124.5 %all-reduce.4.cloned.1.call-start = ((), (), s32[]{:S(2)}) async-start(), calls=%async_computation.1 | async-start | bytes 1351680 | tf_op jit(solution)/shard_map/psum | solution.py:53
  15.6 10.6 %copy-start.2 = (s32[32,3072]{1,0:T(8,128)S(1)}, s32[32,3072]{1,0:T(8,128)}, u32[]{:S(2)}) copy-start(s32[32,3072]{1,0:T(8,128)} %param.4) | copy-start | bytes 1179652
  26.1 16.0 %copy-start.1 = (f32[32,3072]{1,0:T(8,128)S(1)}, f32[32,3072]{1,0:T(8,128)}, u32[]{:S(2)}) copy-start(f32[32,3072]{1,0:T(8,128)} %param.5) | copy-start | bytes 1179652
  26.1 16.0 %copy-start.4 = (s32[32,3072]{1,0:T(8,128)S(1)}, s32[32,3072]{1,0:T(8,128)}, u32[]{:S(2)}) copy-start(s32[32,3072]{1,0:T(8,128)} %param.3) | copy-start | bytes 1179652
  131.1 9.1 %copy-start.3 = (f32[33,33,32]{2,0,1:T(8,128)S(1)}, f32[33,33,32]{2,0,1:T(8,128)}, u32[]{:S(2)}) copy-start(f32[33,33,32]{2,0,1:T(8,128)} %all-reduce.4.cloned.1.call-done) | copy-start | bytes 418180
  155.7 89.0 %all-to-all-start = ((bf16[16,2,32,3072]{3,2,1,0:T(8,128)(2,1)}), bf16[16,2,32,3072]{3,2,1,0:T(8,128)(2,1)}, u32[]{:S(2)}, u32[]{:S(2)}) async-start(bf16[16,2,32,3072]{3,2,1,0:T(8,128)(2,1)} %stack.170), calls=%async_computation | async-start | bytes 12582912 | tf_op jit(solution)/shard_map/all_to_all | solution.py:71
  160.3 190.6 %all-reduce.6.cloned.1.call-start = ((), (), s32[]{:S(2)}) async-start(), calls=%async_computation.2 | async-start | bytes 6291456 | tf_op jit(solution)/shard_map/psum | solution.py:9
  247.9 2.7 copy-start
  350.9 11.7 %copy-start.5 = (bf16[2,512,1536]{2,1,0:T(8,128)(2,1)S(1)}, bf16[2,512,1536]{2,1,0:T(8,128)(2,1)}, u32[]{:S(2)}) copy-start(bf16[2,512,1536]{2,1,0:T(8,128)(2,1)} %all-reduce.6.cloned.1.call-done) | copy-start | bytes 9437188
Sparse Core Ops, SparseCore 0:
  41.9 89.1 all-reduce.3
  253.2 97.6 all-reduce.5
